TPU v7x, 256 devices: a whole 4x4x8 slice. The times are simulated.
256 devices in a mesh: group: 32 (over y_hi, z, core), tok: 8 (over x, y_lo).
Axes of the slice: x: 4, y: 4 (y_hi: 2, y_lo: 2; y = y_hi * 2 + y_lo), z: 8, core: 2. Of those that a mesh axis runs over, the one named last changes fastest.
Arguments:
- latents: bfloat16 [32768, 5120], P(('group', 'tok')), may hold values from -6 to 6
- timesteps: int32 [32], P('group'), may hold values from 0 to 999
- mod_shift: float32 [5120], replicated, may hold values from -3 to 3
- mod_scale: float32 [5120], replicated, may hold values from -1.5 to 1.5
- w_query: bfloat16 [5120, 3072], P('group', 'tok'), may hold values from -7 to 7
- w_key: bfloat16 [5120, 3072], P('group', 'tok'), may hold values from -7 to 7
- w_value: bfloat16 [5120, 3072], P('group', 'tok'), may hold values from -0.078125 to 0.078125
- query_gain: float32 [3072], P('tok'), may hold values from 0.5 to 1.5
- key_gain: float32 [3072], P('tok'), may hold values from 0.5 to 1.5
- cache_keys: bfloat16 [32768, 3072], P('group', 'tok'), may hold values from -85 to 85
- cache_values: bfloat16 [32768, 3072], P('group', 'tok'), may hold values from -6 to 6
- owners: int32 [32], replicated, may hold values from 0 to 31, each once
- tile_mask: int32 [24, 8, 24], P('tok'), may hold values from 0 to 1, as said below
Outputs:
- attended: bfloat16 [32768, 3072], P('group', 'tok')
Inputs may be any that keep to these rules, and one draw needn't show every extreme that they name: `tile_mask`: each query tile i of each head sees 1 to 8 key tiles, always tile 2 * 8 + i; some query tile sees exactly 8.
All inputs are finite; a program needn't handle non-finite values.
Results may differ from a plain program's by a relative error of at most 0.012.
The roundings to bfloat16 on the way count: a program that leaves them out, or rounds other values in their place, can miss the bound.
Values may be sent and summed in bfloat16 or wider, within the bound.
No kernel may reach another device: no remote copies, remote signals or barrier semaphores. Data moves between devices by JAX's collectives and lax.ppermute only.
A program may use at most 128 MiB of HBM per device.

v0:
```python
import math
import jax
import jax.numpy as jnp
from jax import lax
from jax.sharding import PartitionSpec as P

EPSILON = 1e-06


def from_behind(block, axis, distance):
    devices = range(lax.axis_size(axis))
    route = [(i - distance, i) for i in devices if i - distance in devices]
    return lax.ppermute(block, axis, route)


def spread_2(value, axis, source):
    kept = jnp.where(lax.axis_index(axis) == source, value, 0).astype(value.dtype)
    return lax.psum(kept, axis)


def modulate(rows_block, timestep, mod_shift, mod_scale):
    values = rows_block.astype(jnp.float32)
    width = values.shape[-1]
    centred = values - jnp.mean(values, axis=-1, keepdims=True)
    spread = jnp.mean(centred * centred, axis=-1, keepdims=True)
    normed = centred * lax.rsqrt(spread + EPSILON)
    freqs = jnp.exp(-math.log(10000.0) * jnp.arange(width, dtype=jnp.float32) / width)
    angles = timestep.astype(jnp.float32) * freqs
    return (
        normed * (1.0 + mod_scale + 0.5 * jnp.cos(angles)) + mod_shift + 0.5 * jnp.sin(angles)
    ).astype(jnp.bfloat16)


def scaled_rows(raw, squares, width, gain):
    return (raw * lax.rsqrt(squares / width + EPSILON)[:, None] * gain).astype(jnp.bfloat16)


def listed_attention(query_tiles, key_tiles, value_tiles, allowed, score_scale):
    key_tile_count = allowed.shape[2]
    active_count = jnp.sum(allowed, axis=-1)
    tile_order = jnp.argsort(1 - allowed, axis=-1, stable=True)
    visits = min(8, key_tile_count)
    tile_shape = query_tiles.shape
    tile_ids = jnp.arange(key_tile_count, dtype=jnp.int32)
    start_max = jnp.full(tile_shape[:3], -1e30, jnp.float32)
    start_sum = jnp.zeros(tile_shape[:3], jnp.float32)
    start_acc = jnp.zeros(tile_shape, jnp.float32)

    def visit(visit_index, carry):
        running_max, running_sum, accumulated = carry
        picked = lax.dynamic_index_in_dim(tile_order, visit_index, 2, keepdims=False)
        selector = (picked[:, :, None] == tile_ids[None, None, :]).astype(jnp.bfloat16)
        key_tile = jnp.einsum(
            "hqk,hkjd->hqjd", selector, key_tiles, preferred_element_type=jnp.float32
        ).astype(jnp.bfloat16)
        value_tile = jnp.einsum(
            "hqk,hkjd->hqjd", selector, value_tiles, preferred_element_type=jnp.float32
        ).astype(jnp.bfloat16)
        scores = (
            jnp.einsum("hqid,hqjd->hqij", query_tiles, key_tile, preferred_element_type=jnp.float32)
            * score_scale
        )
        is_live = (visit_index < active_count)[:, :, None]
        new_max = jnp.where(
            is_live, jnp.maximum(running_max, jnp.max(scores, axis=-1)), running_max
        )
        shrink = jnp.exp(running_max - new_max)
        weights = jnp.exp(scores - new_max[..., None])
        new_sum = jnp.where(is_live, running_sum * shrink + jnp.sum(weights, axis=-1), running_sum)
        added = jnp.einsum(
            "hqij,hqjd->hqid",
            weights.astype(jnp.bfloat16),
            value_tile,
            preferred_element_type=jnp.float32,
        )
        new_acc = jnp.where(
            is_live[..., None], accumulated * shrink[..., None] + added, accumulated
        )
        return (new_max, new_sum, new_acc)

    final_max, final_sum, final_acc = lax.fori_loop(
        0, visits, visit, (start_max, start_sum, start_acc)
    )
    return (final_acc / final_sum[..., None]).astype(jnp.bfloat16)


def local(
    latents,
    timesteps,
    mod_shift,
    mod_scale,
    w_query,
    w_key,
    w_value,
    query_gain,
    key_gain,
    cache_keys,
    cache_values,
    owners,
    tile_mask,
):
    modulated = modulate(latents, timesteps[0], mod_shift, mod_scale)
    root = owners[owners.shape[0] - 1]
    head_cols = w_query.shape[1]
    slabs = (
        lax.all_gather(w_query, "group", axis=0, tiled=True),
        lax.all_gather(w_key, "group", axis=0, tiled=True),
        lax.all_gather(w_value, "group", axis=0, tiled=True),
    )
    joined = jnp.concatenate(slabs, axis=1)
    projected = jnp.dot(
        lax.all_gather(modulated, "tok", axis=0, tiled=True),
        joined,
        preferred_element_type=jnp.float32,
    )
    raw_query = projected[:, :head_cols]
    raw_key = projected[:, head_cols : 2 * head_cols]
    raw_value = projected[:, 2 * head_cols :]
    query_squares, key_squares = lax.psum(
        (jnp.sum(raw_query * raw_query, axis=1), jnp.sum(raw_key * raw_key, axis=1)), "tok"
    )
    width = head_cols * lax.axis_size("tok")
    query_rows = scaled_rows(raw_query, query_squares, width, query_gain)
    key_rows = scaled_rows(raw_key, key_squares, width, key_gain)
    value_rows = raw_value.astype(jnp.bfloat16)
    earlier_keys, earlier_values = from_behind((key_rows, value_rows), "group", 1)
    cached = (spread_2(cache_keys, "group", root), spread_2(cache_values, "group", root))
    group_rows = query_rows.shape[0]
    local_heads = tile_mask.shape[0]
    query_tiles = tile_mask.shape[1]
    key_tile_count = tile_mask.shape[2]
    tile_rows = group_rows // query_tiles
    head_size = head_cols // local_heads
    score_scale = 1.0 / math.sqrt(head_size)
    context_keys = jnp.concatenate([cached[0], earlier_keys, key_rows], axis=0)
    context_values = jnp.concatenate([cached[1], earlier_values, value_rows], axis=0)
    is_first = lax.axis_index("group") == 0
    tile_ids = jnp.arange(key_tile_count, dtype=jnp.int32)
    earlier_region = (tile_ids >= query_tiles) & (tile_ids < 2 * query_tiles)
    allowed = jnp.where(earlier_region[None, None, :] & is_first, 0, tile_mask)
    query_heads = query_rows.reshape(group_rows, local_heads, head_size).transpose(1, 0, 2)
    key_heads = context_keys.reshape(3 * group_rows, local_heads, head_size).transpose(1, 0, 2)
    value_heads = context_values.reshape(3 * group_rows, local_heads, head_size).transpose(1, 0, 2)
    attended = listed_attention(
        query_heads.reshape(local_heads, query_tiles, tile_rows, head_size),
        key_heads.reshape(local_heads, key_tile_count, tile_rows, head_size),
        value_heads.reshape(local_heads, key_tile_count, tile_rows, head_size),
        allowed,
        score_scale,
    ).reshape(local_heads, group_rows, head_size)
    return attended.transpose(1, 0, 2).reshape(group_rows, head_cols)


def solution(mesh):
    return jax.shard_map(
        local,
        mesh=mesh,
        in_specs=(
            P(("group", "tok"), None),
            P("group"),
            P(),
            P(),
            P("group", "tok"),
            P("group", "tok"),
            P("group", "tok"),
            P("tok"),
            P("tok"),
            P("group", "tok"),
            P("group", "tok"),
            P(),
            P("tok", None, None),
        ),
        out_specs=P("group", "tok"),
        check_vma=False,
    )
```

profile of v0, /device:TPU:1, one launch (start us, length us, event | category | flops | bytes accessed | tf_op | source)
XLA Modules:
  0.0 861.7 jit_solution(1480350413721025981)
XLA Ops:
  16.2 83.9 %all-gather.11.cloned.1.call-done = bf16[5120,384]{1,0:T(8,128)(2,1)} async-done(((bf16[160,384]{1,0:T(8,128)(2,1)}), bf16[5120,384]{1,0:T(8,128)(2,1)}) %all-gather.11.cloned.1.call-update) | async-done | bytes 3932176 | tf_op jit(solution)/shard_map/all_gather | solution.py:108
  100.1 85.2 %all-gather.7.cloned.1.call-done = bf16[5120,384]{1,0:T(8,128)(2,1)} async-done(((bf16[160,384]{1,0:T(8,128)(2,1)}), bf16[5120,384]{1,0:T(8,128)(2,1)}) %all-gather.7.cloned.1.call-update) | async-done | bytes 3932176 | tf_op jit(solution)/shard_map/all_gather | solution.py:106
  185.3 85.3 %all-gather.9.cloned.1.call-done = bf16[5120,384]{1,0:T(8,128)(2,1)} async-done(((bf16[160,384]{1,0:T(8,128)(2,1)}), bf16[5120,384]{1,0:T(8,128)(2,1)}) %all-gather.9.cloned.1.call-update) | async-done | bytes 3932176 | tf_op jit(solution)/shard_map/all_gather | solution.py:107
  270.6 208.0 %all-gather.5.cloned.1.call-done = bf16[1024,5120]{1,0:T(8,128)(2,1)} async-done(((bf16[128,5120]{1,0:T(8,128)(2,1)}), bf16[1024,5120]{1,0:T(8,128)(2,1)}) %all-gather.5.cloned.1.call-update) | async-done | bytes 10485776 | tf_op jit(solution)/shard_map/all_gather | solution.py:112
  478.6 24.9 %fusion.16 = f32[1024,1152]{1,0:T(8,128)S(1)} fusion(bf16[1024,5120]{1,0:T(8,128)(2,1)} %all-gather.5.cloned.1.call-done, bf16[5120,384]{1,0:T(8,128)(2,1)} %all-gather.11.cloned.1.call-done, bf16[5120,384]{1,0:T(8,128)(2,1)} %all-gather.9.cloned.1.call-done, bf16[5120,384]{1,0:T(8,128)(2,1)} %all-gather.7.cloned.1.call-done), kind=kOutput, calls=%fused_computation.25 | convolution fusion | flops 12114984960 | bytes 27000832 | tf_op jit(solution)/shard_map/dot_general | solution.py:111
  505.9 16.9 %all-reduce = (f32[1024]{0:T(1024)S(1)}, f32[1024]{0:T(1024)S(1)}) all-reduce(f32[1024]{0:T(1024)S(1)} %get-tuple-element.221, f32[1024]{0:T(1024)S(1)} %get-tuple-element.220), channel_id=1, replica_groups=mesh['group'=32,'tok'=8] {'tok'}, use_global_device_ids=true, to_apply=%region_5.0 | all-reduce | flops 2048 | bytes 16384 | tf_op jit(solution)/shard_map/psum | solution.py:119
  526.3 6.9 collective-permute-start
  541.2 215.3 %all-reduce.4.cloned.1.call-done = (bf16[1024,384]{1,0:T(8,128)(2,1)}, bf16[1024,384]{1,0:T(8,128)(2,1)}) async-done(((bf16[1024,384]{1,0:T(8,128)(2,1)}, bf16[1024,384]{1,0:T(8,128)(2,1)}), (bf16[1024,384]{1,0:T(8,128)(2,1)}, bf16[1024,384]{1,0:T(8,128)(2,1)})) %all-reduce.4.cloned.1.call-update) | async-done | bytes 1572880 | tf_op jit(solution)/shard_map/psum | solution.py:18
  759.7 4.3 copy.21
  764.0 4.4 copy.36
  771.1 4.3 copy.23
  775.4 4.3 copy.38
  779.7 73.5 %while.18 = (s32[]{:T(128)}, f32[3,8,128]{2,1,0:T(8,128)S(1)}, f32[3,8,128]{2,1,0:T(8,128)S(1)}, f32[3,8,128,128]{3,2,1,0:T(8,128)S(1)}, s32[3,8]{1,0:T(4,128)S(...) while((s32[]{:T(128)}, f32[3,8,128]{2,1,0:T(8,128)S(1)}, ...), condition=%wide.region_13.14_spmd.clone, body=%wide.region_10.13_spmd.clone.sunk | while | flops 243030176 | bytes 19858332 | solution.py:81
  779.7 3.5 fusion.47
  784.3 3.4 fusion.49
  788.9 3.5 fusion.47
  793.5 3.4 fusion.49
  798.1 3.5 fusion.47
  802.7 3.4 fusion.49
  807.3 3.5 fusion.47
  816.5 3.5 fusion.47
  825.7 3.5 fusion.47
  834.9 3.5 fusion.47
  844.1 3.5 fusion.47
  (156 shorter events, 65.0 us)
Async XLA Ops:
  6.5 4.5 copy-start.1
  6.5 5.0 copy-start.7
  6.5 5.2 copy-start.6
  6.5 93.5 %all-gather.11.cloned.1.call-start = ((), (), s32[]{:S(2)}) async-start(), calls=%async_computation.3 | async-start | bytes 4055040 | tf_op jit(solution)/shard_map/all_gather | solution.py:108
  7.3 178.0 %all-gather.7.cloned.1.call-start = ((), (), s32[]{:S(2)}) async-start(), calls=%async_computation.1 | async-start | bytes 4055040 | tf_op jit(solution)/shard_map/all_gather | solution.py:106
  8.0 262.5 %all-gather.9.cloned.1.call-start = ((), (), s32[]{:S(2)}) async-start(), calls=%async_computation.2 | async-start | bytes 4055040 | tf_op jit(solution)/shard_map/all_gather | solution.py:107
  8.7 469.8 %all-gather.5.cloned.1.call-start = ((), (), s32[]{:S(2)}) async-start(), calls=%async_computation | async-start | bytes 11796480 | tf_op jit(solution)/shard_map/all_gather | solution.py:112
  11.5 3.2 copy-start.4
  11.6 3.2 copy-start.5
  13.5 743.0 %all-reduce.4.cloned.1.call-start = ((), (), s32[]{:S(2)}) async-start(), calls=%async_computation.4 | async-start | bytes 3145728 | tf_op jit(solution)/shard_map/psum | solution.py:18
  505.6 17.3 %copy-start.9 = (f32[384]{0:T(512)S(1)}, f32[384]{0:T(512)}, u32[]{:S(2)}) copy-start(f32[384]{0:T(512)} %param.22) | copy-start | bytes 4612
  505.6 17.3 %copy-start.10 = (f32[384]{0:T(512)S(1)}, f32[384]{0:T(512)}, u32[]{:S(2)}) copy-start(f32[384]{0:T(512)} %param.23) | copy-start | bytes 4612
  522.8 14.0 %copy-start.8 = (s32[3,8,24]{2,1,0:T(8,128)S(1)}, s32[3,8,24]{2,1,0:T(8,128)}, u32[]{:S(2)}) copy-start(s32[3,8,24]{2,1,0:T(8,128)} %param.27) | copy-start | bytes 6916
  526.3 230.2 %collective-permute-start = (bf16[1024,384]{1,0:T(8,128)(2,1)}, bf16[1024,384]{1,0:T(8,128)(2,1)}, u32[]{:S(2)}, u32[]{:S(2)}) collective-permute-start(bf16[1024,384]{1,0:T(8,128)(2,1)} %get-tuple-element.249), channel_id=1, source_target_pairs={{0,8},{8,16},{16,24},{24,32},{32,40},{40,48},{48,56},{56,64},{64,7... | collective-permute-start | bytes 2359304 | tf_op jit(solution)/shard_map/ppermute | solution.py:13
  534.6 233.7 %collective-permute-start.1 = (bf16[1024,384]{1,0:T(8,128)(2,1)S(1)}, bf16[1024,384]{1,0:T(8,128)(2,1)}, u32[]{:S(2)}, u32[]{:S(2)}) collective-permute-start(bf16[1024,384]{1,0:T(8,128)(2,1)S(1)} %slice.25), channel_id=1, source_target_pairs={{0,8},{8,16},{16,24},{24,32},{32,40},{40,48},{48,56},{56,64},{64,7... | collective-permute-start | bytes 2359304 | tf_op jit(solution)/shard_map/ppermute | solution.py:13
  764.0 4.4 copy-start.3
  779.7 3.5 copy-start
  788.9 3.5 copy-start
  798.1 3.5 copy-start
  807.3 3.5 copy-start
  816.5 3.5 copy-start
  825.7 3.5 copy-start
  834.9 3.5 copy-start
  844.0 3.5 copy-start
  (2 other events, 4.1 us)
Sparse Core Ops, SparseCore 0:
  10.1 89.9 all-gather.10
  102.8 82.4 all-gather.6
  188.1 82.4 all-gather.8
  272.2 206.3 all-gather.4
  481.1 275.3 all-reduce.3
where the time goes:
time: 863 us; the launch traced here: 862 us
  waiting for transfers between devices  680 us (79%)
  matrix products  94 us (11%)
  local copies, waits for them, and re-layouts  25.7 us (3%)
  other arithmetic  20.9 us (2%)
  blocking collectives  16.9 us (2%)
  between operations  14.7 us (2%)
  starting transfers between devices  9.15 us (1%)
    psum x1, waiting for transfers between devices, spread_2(): return lax.psum(kept, axis)  215 us
    all_gather x1, waiting for transfers between devices, local(): lax.all_gather(modulated, 'tok', axis=0, tiled=True)  208 us
    all_gather x1, waiting for transfers between devices, local(): lax.all_gather(w_key, 'group', axis=0, tiled=True)  85.3 us
    all_gather x1, waiting for transfers between devices, local(): lax.all_gather(w_query, 'group', axis=0, tiled=True)  85.2 us
    all_gather x1, waiting for transfers between devices, local(): lax.all_gather(w_value, 'group', axis=0, tiled=True)  83.9 us
    dot_general x8, matrix products, visit(): jnp.einsum('hqk,hkjd->hqjd', selector, key_tiles, preferred_element_type=...  27.8 us
    dot_general x8, matrix products, visit(): jnp.einsum('hqk,hkjd->hqjd', selector, value_tiles, preferred_element_typ...  27.3 us
    dot_general x1, matrix products, local(): jnp.dot(lax.all_gather(modulated, 'tok', axis=0, tiled=True), joined, pre...  24.9 us
  transfers between devices with their start and end apart: 7, of which 5 were waited for; matrix products, arithmetic and copies ran while one was open for 6% of the time, Pallas kernels for 0%

commit v1 on v0

--- a/solution.py
+++ b/solution.py
@@ -15,7 +15,7 @@
 
 def spread_2(value, axis, source):
     kept = jnp.where(lax.axis_index(axis) == source, value, 0).astype(value.dtype)
-    return lax.psum(kept, axis)
+    return jnp.sum(lax.all_gather(kept, axis), axis=0)
 
 
 def modulate(rows_block, timestep, mod_shift, mod_scale):

time: 863 us -> 957 us (1.11)
  waiting for transfers between devices: 680 us -> 747 us
  other arithmetic: 20.9 us -> 47.3 us
    all_gather x0 -> x2, waiting for transfers between devices: none -> 283 us  [spread_2(): return jnp.sum(lax.all_gather(kept, axis), axis=0)]
    psum x1 -> x0, waiting for transfers between devices: 215 us -> none  [spread_2(): return lax.psum(kept, axis)]
    reduce_sum x0 -> x2, other arithmetic: none -> 25.8 us  [spread_2(): return jnp.sum(lax.all_gather(kept, axis), axis=0)]
  transfers between devices with their start and end apart: 7 -> 8, of which waited for: 5 -> 6; matrix products, arithmetic and copies ran while one was open for 6% -> 8% of each run, Pallas kernels for 0% -> 0%
where the time goes in v1:
time: 957 us; the launch traced here: 956 us
  waiting for transfers between devices  747 us (78%)
  matrix products  94 us (10%)
  other arithmetic  47.3 us (5%)
  local copies, waits for them, and re-layouts  25.7 us (3%)
  blocking collectives  16.8 us (2%)
  between operations  15 us (2%)
    all_gather x2, waiting for transfers between devices, spread_2(): return jnp.sum(lax.all_gather(kept, axis), axis=0)  283 us
    all_gather x1, waiting for transfers between devices, local(): lax.all_gather(modulated, 'tok', axis=0, tiled=True)  208 us
    all_gather x1, waiting for transfers between devices, local(): lax.all_gather(w_value, 'group', axis=0, tiled=True)  85.3 us
    all_gather x1, waiting for transfers between devices, local(): lax.all_gather(w_key, 'group', axis=0, tiled=True)  85.2 us
    all_gather x1, waiting for transfers between devices, local(): lax.all_gather(w_query, 'group', axis=0, tiled=True)  83.2 us
    dot_general x8, matrix products, visit(): jnp.einsum('hqk,hkjd->hqjd', selector, key_tiles, preferred_element_type=...  27.8 us
    dot_general x8, matrix products, visit(): jnp.einsum('hqk,hkjd->hqjd', selector, value_tiles, preferred_element_typ...  27.3 us
    reduce_sum x2, other arithmetic, spread_2(): return jnp.sum(lax.all_gather(kept, axis), axis=0)  25.8 us
  transfers between devices with their start and end apart: 8, of which 6 were waited for; matrix products, arithmetic and copies ran while one was open for 8% of the time, Pallas kernels for 0%

profile of v1, /device:TPU:1, one launch (start us, length us, event | category | flops | bytes accessed | tf_op | source)
XLA Modules:
  0.0 955.6 jit_solution(2095208065799062583)
XLA Ops:
  16.8 83.2 %all-gather.11.cloned.1.call-done = bf16[5120,384]{1,0:T(8,128)(2,1)} async-done(((bf16[160,384]{1,0:T(8,128)(2,1)}), bf16[5120,384]{1,0:T(8,128)(2,1)}) %all-gather.11.cloned.1.call-update) | async-done | bytes 3932176 | tf_op jit(solution)/shard_map/all_gather | solution.py:106
  100.1 85.2 %all-gather.13.cloned.1.call-done = bf16[5120,384]{1,0:T(8,128)(2,1)} async-done(((bf16[160,384]{1,0:T(8,128)(2,1)}), bf16[5120,384]{1,0:T(8,128)(2,1)}) %all-gather.13.cloned.1.call-update) | async-done | bytes 3932176 | tf_op jit(solution)/shard_map/all_gather | solution.py:107
  185.3 85.3 %all-gather.15.cloned.1.call-done = bf16[5120,384]{1,0:T(8,128)(2,1)} async-done(((bf16[160,384]{1,0:T(8,128)(2,1)}), bf16[5120,384]{1,0:T(8,128)(2,1)}) %all-gather.15.cloned.1.call-update) | async-done | bytes 3932176 | tf_op jit(solution)/shard_map/all_gather | solution.py:108
  270.6 208.0 %all-gather.9.cloned.1.call-done = bf16[1024,5120]{1,0:T(8,128)(2,1)} async-done(((bf16[128,5120]{1,0:T(8,128)(2,1)}), bf16[1024,5120]{1,0:T(8,128)(2,1)}) %all-gather.9.cloned.1.call-update) | async-done | bytes 10485776 | tf_op jit(solution)/shard_map/all_gather | solution.py:112
  478.6 24.9 %fusion.16 = f32[1024,1152]{1,0:T(8,128)S(1)} fusion(bf16[1024,5120]{1,0:T(8,128)(2,1)} %all-gather.9.cloned.1.call-done, bf16[5120,384]{1,0:T(8,128)(2,1)} %all-gather.15.cloned.1.call-done, bf16[5120,384]{1,0:T(8,128)(2,1)} %all-gather.13.cloned.1.call-done, bf16[5120,384]{1,0:T(8,128)(2,1)} %all-gather.11.cloned.1.call-done), kind=kOutput, calls=%fused_computation.25 | convolution fusion | flops 12114984960 | bytes 27000832 | tf_op jit(solution)/shard_map/dot_general | solution.py:111
  506.0 16.8 %all-reduce = (f32[1024]{0:T(1024)S(1)}, f32[1024]{0:T(1024)S(1)}) all-reduce(f32[1024]{0:T(1024)S(1)} %get-tuple-element.221, f32[1024]{0:T(1024)S(1)} %get-tuple-element.220), channel_id=1, replica_groups=mesh['group'=32,'tok'=8] {'tok'}, use_global_device_ids=true, to_apply=%region_5.0 | all-reduce | flops 2048 | bytes 16384 | tf_op jit(solution)/shard_map/psum | solution.py:119
  526.3 7.0 collective-permute-start
  541.3 125.2 %all-gather.17.cloned.1.call-done = bf16[32768,384]{1,0:T(8,128)(2,1)} async-done(((bf16[1024,384]{1,0:T(8,128)(2,1)}), bf16[32768,384]{1,0:T(8,128)(2,1)}) %all-gather.17.cloned.1.call-update) | async-done | bytes 25165840 | tf_op jit(solution)/shard_map/all_gather | solution.py:18
  666.5 12.9 %reduce_sum.83 = bf16[1024,384]{1,0:T(8,128)(2,1)S(1)} reduce(bf16[32,1024,384]{2,1,0:T(8,128)(2,1)} %bitcast.58, bf16[]{:T(256)} %constant.80.clone.1), dimensions={0}, to_apply=%region_1.0 | reduce | flops 12189696 | bytes 25952258 | tf_op jit(solution)/shard_map/reduce_sum | solution.py:18
  682.6 4.3 copy.21
  686.9 4.3 copy.36
  691.2 157.8 %all-gather.19.cloned.1.call-done = bf16[32768,384]{1,0:T(8,128)(2,1)} async-done(((bf16[1024,384]{1,0:T(8,128)(2,1)}), bf16[32768,384]{1,0:T(8,128)(2,1)}) %all-gather.19.cloned.1.call-update) | async-done | bytes 25165840 | tf_op jit(solution)/shard_map/all_gather | solution.py:18
  849.0 12.9 %reduce_sum.88 = bf16[1024,384]{1,0:T(8,128)(2,1)S(1)} reduce(bf16[32,1024,384]{2,1,0:T(8,128)(2,1)} %bitcast.57, bf16[]{:T(256)} %constant.80.clone.1), dimensions={0}, to_apply=%region_6.7 | reduce | flops 12189696 | bytes 25952258 | tf_op jit(solution)/shard_map/reduce_sum | solution.py:18
  864.8 4.3 copy.23
  869.0 4.3 copy.38
  873.3 73.5 %while.18 = (s32[]{:T(128)}, f32[3,8,128]{2,1,0:T(8,128)S(1)}, f32[3,8,128]{2,1,0:T(8,128)S(1)}, f32[3,8,128,128]{3,2,1,0:T(8,128)S(1)}, s32[3,8]{1,0:T(4,128)S(...) while((s32[]{:T(128)}, f32[3,8,128]{2,1,0:T(8,128)S(1)}, ...), condition=%wide.region_13.14_spmd.clone, body=%wide.region_10.13_spmd.clone.sunk | while | flops 243030176 | bytes 19858332 | solution.py:81
  873.3 3.5 fusion.47
  882.5 3.5 fusion.47
  891.7 3.5 fusion.47
  900.9 3.5 fusion.47
  910.1 3.5 fusion.47
  919.3 3.5 fusion.47
  928.5 3.5 fusion.47
  937.7 3.5 fusion.47
  (160 shorter events, 75.9 us)
Async XLA Ops:
  6.5 4.5 copy-start.1
  6.5 5.0 copy-start.6
  6.5 5.2 copy-start.5
  6.5 93.5 %all-gather.11.cloned.1.call-start = ((), (), s32[]{:S(2)}) async-start(), calls=%async_computation.1 | async-start | bytes 4055040 | tf_op jit(solution)/shard_map/all_gather | solution.py:106
  7.3 178.0 %all-gather.13.cloned.1.call-start = ((), (), s32[]{:S(2)}) async-start(), calls=%async_computation.2 | async-start | bytes 4055040 | tf_op jit(solution)/shard_map/all_gather | solution.py:107
  8.0 262.5 %all-gather.15.cloned.1.call-start = ((), (), s32[]{:S(2)}) async-start(), calls=%async_computation.3 | async-start | bytes 4055040 | tf_op jit(solution)/shard_map/all_gather | solution.py:108
  8.7 469.8 %all-gather.9.cloned.1.call-start = ((), (), s32[]{:S(2)}) async-start(), calls=%async_computation | async-start | bytes 11796480 | tf_op jit(solution)/shard_map/all_gather | solution.py:112
  11.5 3.2 copy-start.3
  13.4 2.4 copy-start.4
  13.5 653.0 %all-gather.17.cloned.1.call-start = ((), (), s32[]{:S(2)}) async-start(), calls=%async_computation.4 | async-start | bytes 25952256 | tf_op jit(solution)/shard_map/all_gather | solution.py:18
  15.8 833.3 %all-gather.19.cloned.1.call-start = ((), (), s32[]{:S(2)}) async-start(), calls=%async_computation.5 | async-start | bytes 25952256 | tf_op jit(solution)/shard_map/all_gather | solution.py:18
  505.6 17.2 %copy-start.8 = (f32[384]{0:T(512)S(1)}, f32[384]{0:T(512)}, u32[]{:S(2)}) copy-start(f32[384]{0:T(512)} %param.22) | copy-start | bytes 4612
  505.6 17.2 %copy-start.9 = (f32[384]{0:T(512)S(1)}, f32[384]{0:T(512)}, u32[]{:S(2)}) copy-start(f32[384]{0:T(512)} %param.23) | copy-start | bytes 4612
  522.8 14.1 %copy-start.7 = (s32[3,8,24]{2,1,0:T(8,128)S(1)}, s32[3,8,24]{2,1,0:T(8,128)}, u32[]{:S(2)}) copy-start(s32[3,8,24]{2,1,0:T(8,128)} %param.27) | copy-start | bytes 6916
  526.3 153.2 %collective-permute-start = (bf16[1024,384]{1,0:T(8,128)(2,1)}, bf16[1024,384]{1,0:T(8,128)(2,1)}, u32[]{:S(2)}, u32[]{:S(2)}) collective-permute-start(bf16[1024,384]{1,0:T(8,128)(2,1)} %get-tuple-element.247), channel_id=1, source_target_pairs={{0,8},{8,16},{16,24},{24,32},{32,40},{40,48},{48,56},{56,64},{64,7... | collective-permute-start | bytes 2359304 | tf_op jit(solution)/shard_map/ppermute | solution.py:13
  534.8 327.2 %collective-permute-start.1 = (bf16[1024,384]{1,0:T(8,128)(2,1)S(1)}, bf16[1024,384]{1,0:T(8,128)(2,1)}, u32[]{:S(2)}, u32[]{:S(2)}) collective-permute-start(bf16[1024,384]{1,0:T(8,128)(2,1)S(1)} %slice.25), channel_id=1, source_target_pairs={{0,8},{8,16},{16,24},{24,32},{32,40},{40,48},{48,56},{56,64},{64,7... | collective-permute-start | bytes 2359304 | tf_op jit(solution)/shard_map/ppermute | solution.py:13
  873.3 3.5 copy-start
  882.5 3.5 copy-start
  891.7 3.5 copy-start
  900.9 3.5 copy-start
  910.1 3.5 copy-start
  919.3 3.5 copy-start
  928.5 3.5 copy-start
  937.7 3.5 copy-start
  (2 other events, 4.2 us)
Sparse Core Ops, SparseCore 0:
  10.1 89.9 all-gather.10
  102.8 82.4 all-gather.12
  188.1 82.4 all-gather.14
  272.2 206.3 all-gather.8
  481.2 185.2 all-gather.16
  669.1 179.8 all-gather.18
